TPU v7x, 256 devices: a whole 4x4x8 slice. The times are simulated.
256 devices in a mesh: rows: 32 (over x, z_hi, core), cols: 8 (over z_lo, y).
Axes of the slice: x: 4, y: 4, z: 8 (z_hi: 4, z_lo: 2; z = z_hi * 2 + z_lo), core: 2. Of those that a mesh axis runs over, the one named last changes fastest.
Arguments:
- right_side: float32 [4, 8, 1024, 512], P(None, 'cols', 'rows'), may hold values from -6 to 6
- inverse_blocks: bfloat16 [4, 8, 1024, 8192], P(None, None, 'rows', 'cols'), may hold values from -0.09375 to 0.09375
- lower_blocks: bfloat16 [6, 8, 1024, 8192], P(None, None, 'rows', 'cols'), may hold values from -0.046875 to 0.046875
Outputs:
- solution: float32 [4, 8, 1024, 512], P(None, 'cols', 'rows')
All inputs are finite; a program needn't handle non-finite values.
Results may differ from a plain program's by a relative error of at most 0.014.
Values may be sent and summed in bfloat16 or wider, within the bound.
A program may use at most 64 MiB of HBM per device.

v0:
```python
import jax
import jax.numpy as jnp
from jax import lax
from jax.sharding import PartitionSpec as P


def pair_index(target, source):
    return target * (target - 1) // 2 + source


def product(factor_block, rows_all):
    return jnp.einsum("abk,kn->abn", factor_block, rows_all, preferred_element_type=jnp.float32)


def fold_rows(factor_block, incoming):
    return jnp.einsum("abk,kn->abn", factor_block, incoming[0], preferred_element_type=jnp.float32)


def forward_solve(right_side, inverse_blocks, lower_blocks):
    panels = right_side.shape[0]
    groups = inverse_blocks.shape[1]
    local_rows = inverse_blocks.shape[2]
    columns = right_side.shape[3]
    gathered = []
    solutions = []
    for current in range(panels):
        if current == 0:
            residual = right_side[0].astype(jnp.bfloat16)
        else:
            partial_value = jnp.zeros((groups, local_rows, columns), jnp.float32)
            for source in range(current):
                partial_value = partial_value + product(
                    lower_blocks[pair_index(current, source)], gathered[source]
                )
            shares = lax.psum_scatter(partial_value, "cols", scatter_dimension=0, tiled=True)
            residual = (right_side[current] - shares).astype(jnp.bfloat16)
        products = fold_rows(
            inverse_blocks[current], lax.all_gather(residual, "rows", axis=1, tiled=True)
        )
        solved = lax.psum_scatter(products, "cols", scatter_dimension=0, tiled=True)
        solutions.append(solved)
        if current + 1 < panels:
            rows_all = lax.all_gather(solved.astype(jnp.bfloat16), "rows", axis=1, tiled=True)[0]
            gathered.append(rows_all)
    return jnp.stack(solutions)


def body(right_side, inverse_blocks, lower_blocks):
    return forward_solve(right_side, inverse_blocks, lower_blocks)


def solution(mesh):
    return jax.shard_map(
        body,
        mesh=mesh,
        in_specs=(
            P(None, "cols", "rows", None),
            P(None, None, "rows", "cols"),
            P(None, None, "rows", "cols"),
        ),
        out_specs=P(None, "cols", "rows", None),
        check_vma=False,
    )
```

profile of v0, /device:TPU:2, one launch (start us, length us, event | category | flops | bytes accessed | tf_op | source)
XLA Modules:
  0.0 677.7 jit_solution(5792396489258277267)
XLA Ops:
  6.5 1.5 slice.102
  8.1 55.7 %all-gather.21.cloned.1.call-done = bf16[1,1,1024,512]{3,2,1,0:T(8,128)(2,1)} async-done(((bf16[1,1,32,512]{3,2,1,0:T(8,128)(2,1)}), bf16[1,1,1024,512]{3,2,1,0:T(8,128)(2,1)}) %all-gather.21.cloned.1.call-update) | async-done | bytes 1048592 | tf_op jit(solution)/shard_map/all_gather | solution.py:38
  63.8 2.6 fusion.2
  66.5 39.0 %reduce-scatter.8.cloned.1.call-done = f32[1,32,512]{2,1,0:T(8,128)} async-done(((f32[8,32,512]{2,1,0:T(8,128)}), f32[1,32,512]{2,1,0:T(8,128)}) %reduce-scatter.8.cloned.1.call-update) | async-done | bytes 65552 | tf_op jit(solution)/shard_map/reduce_scatter | solution.py:40
  105.5 1.5 convert_element_type.31
  107.0 51.0 %all-gather.9.cloned.1.call-done = bf16[1,1024,512]{2,1,0:T(8,128)(2,1)} async-done(((bf16[1,32,512]{2,1,0:T(8,128)(2,1)}), bf16[1,1024,512]{2,1,0:T(8,128)(2,1)}) %all-gather.9.cloned.1.call-update) | async-done | bytes 1048592 | tf_op jit(solution)/shard_map/all_gather | solution.py:43
  158.1 2.6 convolution_bitcast_fusion.3
  160.7 39.0 %reduce-scatter.10.cloned.1.call-done = f32[1,32,512]{2,1,0:T(8,128)} async-done(((f32[8,32,512]{2,1,0:T(8,128)}), f32[1,32,512]{2,1,0:T(8,128)}) %reduce-scatter.10.cloned.1.call-update) | async-done | bytes 65552 | tf_op jit(solution)/shard_map/reduce_scatter | solution.py:35
  199.8 1.5 fusion.37
  201.3 50.6 %all-gather.11.cloned.1.call-done = bf16[1,1024,512]{2,1,0:T(8,128)(2,1)} async-done(((bf16[1,32,512]{2,1,0:T(8,128)(2,1)}), bf16[1,1024,512]{2,1,0:T(8,128)(2,1)}) %all-gather.11.cloned.1.call-update) | async-done | bytes 1048592 | tf_op jit(solution)/shard_map/all_gather | solution.py:38
  251.9 2.5 convolution_bitcast_fusion.2
  254.4 39.0 %reduce-scatter.12.cloned.1.call-done = f32[1,32,512]{2,1,0:T(8,128)} async-done(((f32[8,32,512]{2,1,0:T(8,128)}), f32[1,32,512]{2,1,0:T(8,128)}) %reduce-scatter.12.cloned.1.call-update) | async-done | bytes 65552 | tf_op jit(solution)/shard_map/reduce_scatter | solution.py:40
  293.5 1.5 convert_element_type.33
  295.0 1.8 fusion.12
  296.8 49.2 %all-gather.13.cloned.1.call-done = bf16[1,1024,512]{2,1,0:T(8,128)(2,1)} async-done(((bf16[1,32,512]{2,1,0:T(8,128)(2,1)}), bf16[1,1024,512]{2,1,0:T(8,128)(2,1)}) %all-gather.13.cloned.1.call-update) | async-done | bytes 1048592 | tf_op jit(solution)/shard_map/all_gather | solution.py:43
  346.0 2.6 fusion.1
  348.7 39.1 %reduce-scatter.14.cloned.1.call-done = f32[1,32,512]{2,1,0:T(8,128)} async-done(((f32[8,32,512]{2,1,0:T(8,128)}), f32[1,32,512]{2,1,0:T(8,128)}) %reduce-scatter.14.cloned.1.call-update) | async-done | bytes 65552 | tf_op jit(solution)/shard_map/reduce_scatter | solution.py:35
  387.7 1.5 fusion.36
  389.3 50.7 %all-gather.15.cloned.1.call-done = bf16[1,1024,512]{2,1,0:T(8,128)(2,1)} async-done(((bf16[1,32,512]{2,1,0:T(8,128)(2,1)}), bf16[1,1024,512]{2,1,0:T(8,128)(2,1)}) %all-gather.15.cloned.1.call-update) | async-done | bytes 1048592 | tf_op jit(solution)/shard_map/all_gather | solution.py:38
  439.9 2.5 convolution_bitcast_fusion.1
  442.5 39.0 %reduce-scatter.16.cloned.1.call-done = f32[1,32,512]{2,1,0:T(8,128)} async-done(((f32[8,32,512]{2,1,0:T(8,128)}), f32[1,32,512]{2,1,0:T(8,128)}) %reduce-scatter.16.cloned.1.call-update) | async-done | bytes 65552 | tf_op jit(solution)/shard_map/reduce_scatter | solution.py:40
  481.5 1.5 convert_element_type.35
  483.0 1.8 fusion.10
  484.8 1.8 convolution_add_fusion.1
  486.6 47.4 %all-gather.17.cloned.1.call-done = bf16[1,1024,512]{2,1,0:T(8,128)(2,1)} async-done(((bf16[1,32,512]{2,1,0:T(8,128)(2,1)}), bf16[1,1024,512]{2,1,0:T(8,128)(2,1)}) %all-gather.17.cloned.1.call-update) | async-done | bytes 1048592 | tf_op jit(solution)/shard_map/all_gather | solution.py:43
  534.0 2.6 fusion
  536.7 39.0 %reduce-scatter.18.cloned.1.call-done = f32[1,32,512]{2,1,0:T(8,128)} async-done(((f32[8,32,512]{2,1,0:T(8,128)}), f32[1,32,512]{2,1,0:T(8,128)}) %reduce-scatter.18.cloned.1.call-update) | async-done | bytes 65552 | tf_op jit(solution)/shard_map/reduce_scatter | solution.py:35
  575.7 1.5 fusion.35
  577.2 50.7 %all-gather.19.cloned.1.call-done = bf16[1,1024,512]{2,1,0:T(8,128)(2,1)} async-done(((bf16[1,32,512]{2,1,0:T(8,128)(2,1)}), bf16[1,1024,512]{2,1,0:T(8,128)(2,1)}) %all-gather.19.cloned.1.call-update) | async-done | bytes 1048592 | tf_op jit(solution)/shard_map/all_gather | solution.py:38
  628.0 2.5 convolution_bitcast_fusion
  630.5 39.1 %reduce-scatter.20.cloned.1.call-done = f32[1,32,512]{2,1,0:T(8,128)} async-done(((f32[8,32,512]{2,1,0:T(8,128)}), f32[1,32,512]{2,1,0:T(8,128)}) %reduce-scatter.20.cloned.1.call-update) | async-done | bytes 65552 | tf_op jit(solution)/shard_map/reduce_scatter | solution.py:40
  669.6 1.6 pad_maximum_fusion
  (38 shorter events, 0.8 us)
Async XLA Ops:
  6.5 57.2 %all-gather.21.cloned.1.call-start = ((), (), s32[]{:S(2)}) async-start(), calls=%async_computation.20 | async-start | bytes 1081344 | tf_op jit(solution)/shard_map/all_gather | solution.py:38
  8.0 191.7 %copy-start.3 = (f32[4,1,32,512]{3,2,1,0:T(8,128)S(1)}, f32[4,1,32,512]{3,2,1,0:T(8,128)}, u32[]{:S(2)}) copy-start(f32[4,1,32,512]{3,2,1,0:T(8,128)} %param.3) | copy-start | bytes 786436
  8.0 97.5 %reduce-scatter.8.cloned.1.call-start = ((), (), s32[]{:S(2)}) async-start(), calls=%async_computation.7 | async-start | bytes 589824 | tf_op jit(solution)/shard_map/reduce_scatter | solution.py:40
  66.4 185.5 %copy-start.4 = (bf16[4,8,32,1024]{3,2,1,0:T(8,128)(2,1)S(1)}, bf16[4,8,32,1024]{3,2,1,0:T(8,128)(2,1)}, u32[]{:S(2)}) copy-start(bf16[4,8,32,1024]{3,2,1,0:T(8,128)(2,1)} %param.4) | copy-start | bytes 6291460
  66.4 91.6 %all-gather.9.cloned.1.call-start = ((), (), s32[]{:S(2)}) async-start(), calls=%async_computation.8 | async-start | bytes 1081344 | tf_op jit(solution)/shard_map/all_gather | solution.py:43
  107.0 92.8 %reduce-scatter.10.cloned.1.call-start = ((), (), s32[]{:S(2)}) async-start(), calls=%async_computation.9 | async-start | bytes 589824 | tf_op jit(solution)/shard_map/reduce_scatter | solution.py:35
  160.7 91.2 %all-gather.11.cloned.1.call-start = ((), (), s32[]{:S(2)}) async-start(), calls=%async_computation.10 | async-start | bytes 1081344 | tf_op jit(solution)/shard_map/all_gather | solution.py:38
  201.2 92.2 %reduce-scatter.12.cloned.1.call-start = ((), (), s32[]{:S(2)}) async-start(), calls=%async_computation.11 | async-start | bytes 589824 | tf_op jit(solution)/shard_map/reduce_scatter | solution.py:40
  254.4 91.6 %all-gather.13.cloned.1.call-start = ((), (), s32[]{:S(2)}) async-start(), calls=%async_computation.12 | async-start | bytes 1081344 | tf_op jit(solution)/shard_map/all_gather | solution.py:43
  295.0 92.8 %reduce-scatter.14.cloned.1.call-start = ((), (), s32[]{:S(2)}) async-start(), calls=%async_computation.13 | async-start | bytes 589824 | tf_op jit(solution)/shard_map/reduce_scatter | solution.py:35
  348.6 91.3 %all-gather.15.cloned.1.call-start = ((), (), s32[]{:S(2)}) async-start(), calls=%async_computation.14 | async-start | bytes 1081344 | tf_op jit(solution)/shard_map/all_gather | solution.py:38
  389.2 92.3 %reduce-scatter.16.cloned.1.call-start = ((), (), s32[]{:S(2)}) async-start(), calls=%async_computation.15 | async-start | bytes 589824 | tf_op jit(solution)/shard_map/reduce_scatter | solution.py:40
  442.4 91.6 %all-gather.17.cloned.1.call-start = ((), (), s32[]{:S(2)}) async-start(), calls=%async_computation.16 | async-start | bytes 1081344 | tf_op jit(solution)/shard_map/all_gather | solution.py:43
  483.0 92.8 %reduce-scatter.18.cloned.1.call-start = ((), (), s32[]{:S(2)}) async-start(), calls=%async_computation.17 | async-start | bytes 589824 | tf_op jit(solution)/shard_map/reduce_scatter | solution.py:35
  536.6 132.9 %copy-start = (f32[1,32,512]{2,1,0:T(8,128)S(1)}, f32[1,32,512]{2,1,0:T(8,128)}, u32[]{:S(2)}) copy-start(f32[1,32,512]{2,1,0:T(8,128)} %reduce-scatter.8.cloned.1.call-done) | copy-start | bytes 196612
  536.6 132.9 %copy-start.1 = (f32[1,32,512]{2,1,0:T(8,128)S(1)}, f32[1,32,512]{2,1,0:T(8,128)}, u32[]{:S(2)}) copy-start(f32[1,32,512]{2,1,0:T(8,128)} %reduce-scatter.12.cloned.1.call-done) | copy-start | bytes 196612
  536.6 132.9 %copy-start.2 = (f32[1,32,512]{2,1,0:T(8,128)S(1)}, f32[1,32,512]{2,1,0:T(8,128)}, u32[]{:S(2)}) copy-start(f32[1,32,512]{2,1,0:T(8,128)} %reduce-scatter.16.cloned.1.call-done) | copy-start | bytes 196612
  536.7 91.3 %all-gather.19.cloned.1.call-start = ((), (), s32[]{:S(2)}) async-start(), calls=%async_computation.18 | async-start | bytes 1081344 | tf_op jit(solution)/shard_map/all_gather | solution.py:38
  577.2 92.4 %reduce-scatter.20.cloned.1.call-start = ((), (), s32[]{:S(2)}) async-start(), calls=%async_computation.19 | async-start | bytes 589824 | tf_op jit(solution)/shard_map/reduce_scatter | solution.py:40
Sparse Core Ops, SparseCore 0:
  9.9 53.8 all-gather.20
  66.6 38.8 reduce-scatter.7
  108.4 49.6 all-gather.8
  160.8 38.8 reduce-scatter.9
  202.2 49.6 all-gather.10
  254.5 38.9 reduce-scatter.11
  296.3 49.5 all-gather.12
  348.7 38.9 reduce-scatter.13
  390.3 49.5 all-gather.14
  442.5 38.8 reduce-scatter.15
  484.4 49.6 all-gather.16
  536.8 38.8 reduce-scatter.17
  578.3 49.6 all-gather.18
  630.6 38.9 reduce-scatter.19
where the time goes:
time: 678 us
  waiting for transfers between devices  629 us (93%)
  matrix products  23.2 us (3%)
  between operations  13.3 us (2%)
  other arithmetic  10.3 us (2%)
    all_gather x4, waiting for transfers between devices, forward_solve(): lax.all_gather(residual, 'rows', axis=1, tiled=True)  208 us
    reduce_scatter x4, waiting for transfers between devices, forward_solve(): solved = lax.psum_scatter(products, 'cols', scatter_dimension=0, tiled=True)  156 us
    all_gather x3, waiting for transfers between devices, forward_solve(): lax.all_gather(solved.astype(jnp.bfloat16), 'rows', axis=1, tiled=True)[0]  148 us
    reduce_scatter x3, waiting for transfers between devices, forward_solve(): lax.psum_scatter(partial_value, 'cols', scatter_dimension=0, tiled=True)  117 us
  transfers between devices with their start and end apart: 14, of which 14 were waited for; matrix products, arithmetic and copies ran while one was open for 1% of the time, Pallas kernels for 0%

commit v1 on v0

--- a/solution.py
+++ b/solution.py
@@ -35,7 +35,10 @@
             shares = lax.psum_scatter(partial_value, "cols", scatter_dimension=0, tiled=True)
             residual = (right_side[current] - shares).astype(jnp.bfloat16)
         products = fold_rows(
-            inverse_blocks[current], lax.all_gather(residual, "rows", axis=1, tiled=True)
+            inverse_blocks[current],
+            jnp.concatenate(
+                lax.all_to_all(jnp.stack([residual] * lax.axis_size("rows")), "rows", 0, 0), axis=1
+            ),
         )
         solved = lax.psum_scatter(products, "cols", scatter_dimension=0, tiled=True)
         solutions.append(solved)

time: 678 us -> 606 us (0.89)
  waiting for transfers between devices: 629 us -> 424 us
  blocking collectives: 0 us -> 139 us
    all_gather x4 -> x0, waiting for transfers between devices: 208 us -> none  [forward_solve(): lax.all_gather(residual, 'rows', axis=1, tiled=True)]
    all_to_all x0 -> x4, blocking collectives: none -> 139 us  [forward_solve(): lax.all_to_all(jnp.stack([residual] * lax.axis_size('rows')), 'rows', 0, 0)]
  transfers between devices with their start and end apart: 14 -> 10, of which waited for: 14 -> 10; matrix products, arithmetic and copies ran while one was open for 1% -> 1% of each run, Pallas kernels for 0% -> 0%
where the time goes in v1:
time: 606 us; the launch traced here: 605 us
  waiting for transfers between devices  424 us (70%)
  blocking collectives  139 us (23%)
  matrix products  18.3 us (3%)
  between operations  13.7 us (2%)
  other arithmetic  8.49 us (1%)
    reduce_scatter x4, waiting for transfers between devices, forward_solve(): solved = lax.psum_scatter(products, 'cols', scatter_dimension=0, tiled=True)  159 us
    all_gather x3, waiting for transfers between devices, forward_solve(): lax.all_gather(solved.astype(jnp.bfloat16), 'rows', axis=1, tiled=True)[0]  148 us
    all_to_all x4, blocking collectives, forward_solve(): lax.all_to_all(jnp.stack([residual] * lax.axis_size('rows')), 'rows', 0, 0)  139 us
    reduce_scatter x3, waiting for transfers between devices, forward_solve(): lax.psum_scatter(partial_value, 'cols', scatter_dimension=0, tiled=True)  117 us
    dot_general x6, matrix products, product(): jnp.einsum('abk,kn->abn', factor_block, rows_all, preferred_element_type=...  13.3 us
  transfers between devices with their start and end apart: 10, of which 10 were waited for; matrix products, arithmetic and copies ran while one was open for 1% of the time, Pallas kernels for 0%

profile of v1, /device:TPU:2, one launch (start us, length us, event | category | flops | bytes accessed | tf_op | source)
XLA Modules:
  0.0 605.1 jit_solution(910487825803751694)
XLA Ops:
  6.5 1.0 fusion.37
  7.7 39.1 %all_to_all.20 = bf16[32,1,32,512]{3,2,1,0:T(8,128)(2,1)S(1)} all-to-all(bf16[32,1,32,512]{3,2,1,0:T(8,128)(2,1)S(1)} %stack.21), channel_id=1, replica_groups=mesh['rows'=32,'cols'=8] {'rows'}, dimensions={0} | all-to-all | bytes 2097152 | tf_op jit(solution)/shard_map/all_to_all | solution.py:40
  46.7 1.3 fusion.19
  48.1 38.2 %reduce-scatter.8.cloned.1.call-done = f32[1,32,512]{2,1,0:T(8,128)} async-done(((f32[8,32,512]{2,1,0:T(8,128)}), f32[1,32,512]{2,1,0:T(8,128)}) %reduce-scatter.8.cloned.1.call-update) | async-done | bytes 65552 | tf_op jit(solution)/shard_map/reduce_scatter | solution.py:43
  86.3 1.5 convert_element_type.28
  87.8 51.0 %all-gather.4.cloned.1.call-done = bf16[1,1024,512]{2,1,0:T(8,128)(2,1)} async-done(((bf16[1,32,512]{2,1,0:T(8,128)(2,1)}), bf16[1,1024,512]{2,1,0:T(8,128)(2,1)}) %all-gather.4.cloned.1.call-update) | async-done | bytes 1048592 | tf_op jit(solution)/shard_map/all_gather | solution.py:46
  138.8 2.6 convolution_bitcast_fusion.3
  141.5 39.0 %reduce-scatter.10.cloned.1.call-done = f32[1,32,512]{2,1,0:T(8,128)} async-done(((f32[8,32,512]{2,1,0:T(8,128)}), f32[1,32,512]{2,1,0:T(8,128)}) %reduce-scatter.10.cloned.1.call-update) | async-done | bytes 65552 | tf_op jit(solution)/shard_map/reduce_scatter | solution.py:35
  180.5 0.9 fusion.34
  181.5 33.3 %all_to_all.21 = bf16[32,1,32,512]{3,2,1,0:T(8,128)(2,1)S(1)} all-to-all(bf16[32,1,32,512]{3,2,1,0:T(8,128)(2,1)S(1)} %stack.23), channel_id=1, replica_groups=mesh['rows'=32,'cols'=8] {'rows'}, dimensions={0} | all-to-all | bytes 2097152 | tf_op jit(solution)/shard_map/all_to_all | solution.py:40
  214.8 1.2 convolution_bitcast_fusion.2
  216.1 40.3 %reduce-scatter.12.cloned.1.call-done = f32[1,32,512]{2,1,0:T(8,128)} async-done(((f32[8,32,512]{2,1,0:T(8,128)}), f32[1,32,512]{2,1,0:T(8,128)}) %reduce-scatter.12.cloned.1.call-update) | async-done | bytes 65552 | tf_op jit(solution)/shard_map/reduce_scatter | solution.py:43
  256.4 1.5 convert_element_type.31
  257.9 2.3 fusion.7
  260.2 48.6 %all-gather.6.cloned.1.call-done = bf16[1,1024,512]{2,1,0:T(8,128)(2,1)} async-done(((bf16[1,32,512]{2,1,0:T(8,128)(2,1)}), bf16[1,1024,512]{2,1,0:T(8,128)(2,1)}) %all-gather.6.cloned.1.call-update) | async-done | bytes 1048592 | tf_op jit(solution)/shard_map/all_gather | solution.py:46
  308.8 2.8 fusion.1
  311.7 39.1 %reduce-scatter.14.cloned.1.call-done = f32[1,32,512]{2,1,0:T(8,128)} async-done(((f32[8,32,512]{2,1,0:T(8,128)}), f32[1,32,512]{2,1,0:T(8,128)}) %reduce-scatter.14.cloned.1.call-update) | async-done | bytes 65552 | tf_op jit(solution)/shard_map/reduce_scatter | solution.py:35
  350.7 0.8 fusion.35
  351.7 33.5 %all_to_all.22 = bf16[32,1,32,512]{3,2,1,0:T(8,128)(2,1)S(1)} all-to-all(bf16[32,1,32,512]{3,2,1,0:T(8,128)(2,1)S(1)} %stack.25), channel_id=1, replica_groups=mesh['rows'=32,'cols'=8] {'rows'}, dimensions={0} | all-to-all | bytes 2097152 | tf_op jit(solution)/shard_map/all_to_all | solution.py:40
  385.2 1.3 convolution_bitcast_fusion.1
  386.5 40.0 %reduce-scatter.16.cloned.1.call-done = f32[1,32,512]{2,1,0:T(8,128)} async-done(((f32[8,32,512]{2,1,0:T(8,128)}), f32[1,32,512]{2,1,0:T(8,128)}) %reduce-scatter.16.cloned.1.call-update) | async-done | bytes 65552 | tf_op jit(solution)/shard_map/reduce_scatter | solution.py:43
  426.5 1.5 convert_element_type.34
  428.0 1.6 fusion.5
  429.6 1.5 convolution_add_fusion.1
  431.1 48.0 %all-gather.8.cloned.1.call-done = bf16[1,1024,512]{2,1,0:T(8,128)(2,1)} async-done(((bf16[1,32,512]{2,1,0:T(8,128)(2,1)}), bf16[1,1024,512]{2,1,0:T(8,128)(2,1)}) %all-gather.8.cloned.1.call-update) | async-done | bytes 1048592 | tf_op jit(solution)/shard_map/all_gather | solution.py:46
  479.0 2.6 fusion
  481.7 39.0 %reduce-scatter.18.cloned.1.call-done = f32[1,32,512]{2,1,0:T(8,128)} async-done(((f32[8,32,512]{2,1,0:T(8,128)}), f32[1,32,512]{2,1,0:T(8,128)}) %reduce-scatter.18.cloned.1.call-update) | async-done | bytes 65552 | tf_op jit(solution)/shard_map/reduce_scatter | solution.py:35
  520.7 0.8 fusion.36
  521.7 33.3 %all_to_all.23 = bf16[32,1,32,512]{3,2,1,0:T(8,128)(2,1)S(1)} all-to-all(bf16[32,1,32,512]{3,2,1,0:T(8,128)(2,1)S(1)} %stack.27), channel_id=1, replica_groups=mesh['rows'=32,'cols'=8] {'rows'}, dimensions={0} | all-to-all | bytes 2097152 | tf_op jit(solution)/shard_map/all_to_all | solution.py:40
  555.1 1.2 convolution_bitcast_fusion
  556.3 40.4 %reduce-scatter.20.cloned.1.call-done = f32[1,32,512]{2,1,0:T(8,128)} async-done(((f32[8,32,512]{2,1,0:T(8,128)}), f32[1,32,512]{2,1,0:T(8,128)}) %reduce-scatter.20.cloned.1.call-update) | async-done | bytes 65552 | tf_op jit(solution)/shard_map/reduce_scatter | solution.py:43
  596.7 1.6 pad_maximum_fusion
  (38 shorter events, 1.0 us)
Async XLA Ops:
  6.5 40.2 %copy-start.4 = (bf16[4,8,32,1024]{3,2,1,0:T(8,128)(2,1)S(1)}, bf16[4,8,32,1024]{3,2,1,0:T(8,128)(2,1)}, u32[]{:S(2)}) copy-start(bf16[4,8,32,1024]{3,2,1,0:T(8,128)(2,1)} %param.4) | copy-start | bytes 6291460
  6.5 79.8 %reduce-scatter.8.cloned.1.call-start = ((), (), s32[]{:S(2)}) async-start(), calls=%async_computation.11 | async-start | bytes 589824 | tf_op jit(solution)/shard_map/reduce_scatter | solution.py:43
  46.7 133.7 %copy-start.3 = (f32[4,1,32,512]{3,2,1,0:T(8,128)S(1)}, f32[4,1,32,512]{3,2,1,0:T(8,128)}, u32[]{:S(2)}) copy-start(f32[4,1,32,512]{3,2,1,0:T(8,128)} %param.3) | copy-start | bytes 786436
  48.0 90.8 %all-gather.4.cloned.1.call-start = ((), (), s32[]{:S(2)}) async-start(), calls=%async_computation.12 | async-start | bytes 1081344 | tf_op jit(solution)/shard_map/all_gather | solution.py:46
  87.8 92.7 %reduce-scatter.10.cloned.1.call-start = ((), (), s32[]{:S(2)}) async-start(), calls=%async_computation.13 | async-start | bytes 589824 | tf_op jit(solution)/shard_map/reduce_scatter | solution.py:35
  141.4 115.0 %reduce-scatter.12.cloned.1.call-start = ((), (), s32[]{:S(2)}) async-start(), calls=%async_computation.14 | async-start | bytes 589824 | tf_op jit(solution)/shard_map/reduce_scatter | solution.py:43
  181.5 76.5 %copy-start.5 = (bf16[1,1024,512]{2,1,0:T(8,128)(2,1)S(1)}, bf16[1,1024,512]{2,1,0:T(8,128)(2,1)}, u32[]{:S(2)}) copy-start(bf16[1,1024,512]{2,1,0:T(8,128)(2,1)} %all-gather.4.cloned.1.call-done) | copy-start | bytes 3145732
  216.0 92.8 %all-gather.6.cloned.1.call-start = ((), (), s32[]{:S(2)}) async-start(), calls=%async_computation.15 | async-start | bytes 1081344 | tf_op jit(solution)/shard_map/all_gather | solution.py:46
  257.9 92.8 %reduce-scatter.14.cloned.1.call-start = ((), (), s32[]{:S(2)}) async-start(), calls=%async_computation.16 | async-start | bytes 589824 | tf_op jit(solution)/shard_map/reduce_scatter | solution.py:35
  311.6 114.9 %reduce-scatter.16.cloned.1.call-start = ((), (), s32[]{:S(2)}) async-start(), calls=%async_computation.17 | async-start | bytes 589824 | tf_op jit(solution)/shard_map/reduce_scatter | solution.py:43
  386.4 92.6 %all-gather.8.cloned.1.call-start = ((), (), s32[]{:S(2)}) async-start(), calls=%async_computation.18 | async-start | bytes 1081344 | tf_op jit(solution)/shard_map/all_gather | solution.py:46
  428.0 92.8 %reduce-scatter.18.cloned.1.call-start = ((), (), s32[]{:S(2)}) async-start(), calls=%async_computation.19 | async-start | bytes 589824 | tf_op jit(solution)/shard_map/reduce_scatter | solution.py:35
  428.0 1.6 copy-start.6
  481.7 115.0 %reduce-scatter.20.cloned.1.call-start = ((), (), s32[]{:S(2)}) async-start(), calls=%async_computation.20 | async-start | bytes 589824 | tf_op jit(solution)/shard_map/reduce_scatter | solution.py:43
  521.7 75.0 %copy-start = (f32[1,32,512]{2,1,0:T(8,128)S(1)}, f32[1,32,512]{2,1,0:T(8,128)}, u32[]{:S(2)}) copy-start(f32[1,32,512]{2,1,0:T(8,128)} %reduce-scatter.8.cloned.1.call-done) | copy-start | bytes 196612
  521.7 75.0 %copy-start.1 = (f32[1,32,512]{2,1,0:T(8,128)S(1)}, f32[1,32,512]{2,1,0:T(8,128)}, u32[]{:S(2)}) copy-start(f32[1,32,512]{2,1,0:T(8,128)} %reduce-scatter.12.cloned.1.call-done) | copy-start | bytes 196612
  521.7 75.0 %copy-start.2 = (f32[1,32,512]{2,1,0:T(8,128)S(1)}, f32[1,32,512]{2,1,0:T(8,128)}, u32[]{:S(2)}) copy-start(f32[1,32,512]{2,1,0:T(8,128)} %reduce-scatter.16.cloned.1.call-done) | copy-start | bytes 196612
Sparse Core Ops, SparseCore 0:
  48.1 38.1 reduce-scatter.7
  89.2 49.6 all-gather.3
  141.6 38.8 reduce-scatter.9
  216.2 40.1 reduce-scatter.11
  259.1 49.6 all-gather.5
  311.7 38.9 reduce-scatter.13
  386.6 39.8 reduce-scatter.15
  429.4 49.6 all-gather.7
  481.8 38.9 reduce-scatter.17
  556.5 40.1 reduce-scatter.19
